TPU v7x, 128 devices: a whole 4x4x4 slice. The times are simulated.
128 devices in a mesh: dom: 16 (over x, y), blk: 8 (over z, core).
Axes of the slice: x: 4, y: 4, z: 4, core: 2. Of those that a mesh axis runs over, the one named last changes fastest.
Arguments:
- node_features: bfloat16 [32768, 512], P(('dom', 'blk')), may hold values from -6 to 6
- norm_gain: float32 [512], replicated, may hold values from 0.25 to 1.75
- w_query: bfloat16 [512, 512], replicated, may hold values from -0.25 to 0.25
- w_key: bfloat16 [512, 512], replicated, may hold values from -0.25 to 0.25
- w_value: bfloat16 [512, 512], replicated, may hold values from -0.25 to 0.25
- w_out: bfloat16 [512, 512], replicated, may hold values from -1.5 to 1.5
- w_message: bfloat16 [512, 512], replicated, may hold values from -1 to 1
- node_cluster: int32 [32768], P(('dom', 'blk')), may hold values from 0 to 15
- block_pattern: int32 [128, 8], P(('dom', 'blk')), may hold values from 0 to 1, as said below
- send_rows: int32 [2048, 128], P(('dom', 'blk')), may hold values from 0 to 255
- send_counts: int32 [2048], P(('dom', 'blk')), may hold values from 32 to 128, as said below
- edge_src: int32 [524288], P(('dom', 'blk')), may hold values from 0 to 2047
- edge_dst: int32 [524288], P(('dom', 'blk')), may hold values from 0 to 255
- out_grad: bfloat16 [32768, 512], P(('dom', 'blk')), may hold values from -6 to 6
Outputs:
- layer_out: bfloat16 [32768, 512], P(('dom', 'blk'))
- feature_grad: bfloat16 [32768, 512], P(('dom', 'blk'))
- weight_grads: float32 [5, 512, 512], replicated
- gain_grad: float32 [512], replicated
Inputs may be any that keep to these rules, and one draw needn't show every extreme that they name: `block_pattern`: row g has a 1 at column (g mod 8); other entries are 0 or 1. `send_counts`: entry g * 16 + p is how many leading slots of device g's block to dom peer p are live; every device has one peer whose block has all 128 slots live.
All inputs are finite; a program needn't handle non-finite values.
Results may differ from a plain program's by a relative error of at most 0.013.
Values may be sent and summed in bfloat16 or wider, within the bound.
No kernel may reach another device: no remote copies, remote signals or barrier semaphores. Data moves between devices by JAX's collectives and lax.ppermute only.
A program may use at most 128 MiB of HBM per device.

v0:
```python
from functools import partial
import jax
import jax.numpy as jnp
from jax import lax
from jax.sharding import PartitionSpec as P

HEADS = 8
HEAD_DIM = 64
epsilon = 1e-06
score_shift = 8.0


def settle(array):
    return lax.optimization_barrier(array.astype(jnp.bfloat16)).astype(jnp.float32)


def rms_norm(features, norm_gain):
    scaling = lax.rsqrt(jnp.mean(features * features, axis=-1, keepdims=True) + epsilon)
    return features * scaling * norm_gain


def head_norm(projected):
    head_view = projected.reshape(projected.shape[0], HEADS, HEAD_DIM)
    scaling = lax.rsqrt(jnp.mean(head_view * head_view, axis=-1, keepdims=True) + epsilon)
    return (head_view * scaling).reshape(projected.shape)


def block_weights(query_heads, key_heads, allowed):
    scaling = score_shift / HEAD_DIM
    scores = (
        jnp.einsum("rhe,khe->hrk", query_heads, key_heads, preferred_element_type=jnp.float32)
        * scaling
    )
    return jnp.where(allowed[None], jnp.exp(scores - score_shift), 0.0)


def attend_piece(running, shard_piece, offset, query_heads, query_labels, pattern_row, skip_empty):
    key_rows, value_rows, key_labels = shard_piece
    row_count = query_heads.shape[0]
    piece_rows = key_rows.shape[0]
    part_count = max(piece_rows // row_count, 1)
    block_index = jnp.arange(pattern_row.shape[0], dtype=jnp.int32)
    for position in range(part_count):
        first_row = position * piece_rows // part_count
        last_row = (position + 1) * piece_rows // part_count
        part_rows = last_row - first_row
        key_part = key_rows[first_row:last_row].reshape(part_rows, HEADS, HEAD_DIM)
        value_part = value_rows[first_row:last_row].reshape(part_rows, HEADS, HEAD_DIM)
        label_part = key_labels[first_row:last_row]
        owners = (offset + first_row + jnp.arange(part_rows, dtype=jnp.int32)) // row_count
        block_flags = jnp.sum(
            jnp.where(owners[:, None] == block_index[None, :], pattern_row[None, :], 0), axis=1
        )
        allowed = (query_labels[:, None] == label_part[None, :]) & (block_flags[None, :] == 1)

        def accumulate(current, key_part=key_part, value_part=value_part, allowed=allowed):
            numer, denom = current
            weights = block_weights(query_heads, key_part, allowed)
            denom = denom + jnp.sum(weights, axis=2).T
            numer = numer + jnp.einsum(
                "hrk,khe->rhe",
                weights.astype(jnp.bfloat16),
                value_part,
                preferred_element_type=jnp.float32,
            )
            return (numer, denom)

        running = accumulate(running)
    return running


def pair_gradients(query_heads, grad_heads, correction, key_part, value_part, allowed):
    scaling = score_shift / HEAD_DIM
    weights = block_weights(query_heads, key_part, allowed)
    grad_dots = jnp.einsum(
        "rhe,khe->hrk", grad_heads, value_part, preferred_element_type=jnp.float32
    )
    slopes = (weights * (grad_dots - correction.T[:, :, None])).astype(jnp.bfloat16)
    dq_part = (
        jnp.einsum("hrk,khe->rhe", slopes, key_part, preferred_element_type=jnp.float32) * scaling
    )
    dk_part = (
        jnp.einsum("hrk,rhe->khe", slopes, query_heads, preferred_element_type=jnp.float32)
        * scaling
    )
    dv_part = jnp.einsum(
        "hrk,rhe->khe", weights.astype(jnp.bfloat16), grad_heads, preferred_element_type=jnp.float32
    )
    return (dq_part, dk_part, dv_part)


def key_block(
    query_heads, grad_heads, correction, query_labels, skip_empty, dq_total, block_inputs
):
    key_part, value_part, label_part, block_flag = block_inputs
    row_count = query_heads.shape[0]
    allowed = (query_labels[:, None] == label_part[None, :]) & (block_flag == 1)
    dq_part, dk_part, dv_part = pair_gradients(
        query_heads, grad_heads, correction, key_part, value_part, allowed
    )
    flat_terms = (dk_part.reshape(row_count, -1), dv_part.reshape(row_count, -1))
    return (dq_total + settle(dq_part), flat_terms)


def local(
    node_features,
    norm_gain,
    w_query,
    w_key,
    w_value,
    w_out,
    w_message,
    node_cluster,
    block_pattern,
    send_rows,
    send_counts,
    edge_src,
    edge_dst,
    out_grad,
):
    row_count = node_features.shape[0]
    feat_width = node_features.shape[1]
    peer_count = lax.axis_size("dom")
    block_count = lax.axis_size("blk")
    slot_count = send_rows.shape[1]
    features = node_features.astype(jnp.float32)
    normed_f, norm_pull = jax.vjp(rms_norm, features, norm_gain)
    normed = normed_f.astype(jnp.bfloat16)
    live_slots = jnp.arange(slot_count, dtype=jnp.int32)[None, :] < send_counts[:, None]
    outgoing = jnp.where(live_slots[:, :, None], normed[send_rows], jnp.zeros((), jnp.bfloat16))
    incoming = lax.all_to_all(outgoing, "dom", split_axis=0, concat_axis=0, tiled=True)
    query_f, query_pull = jax.vjp(
        head_norm, jnp.dot(normed, w_query, preferred_element_type=jnp.float32)
    )
    key_f, key_pull = jax.vjp(head_norm, jnp.dot(normed, w_key, preferred_element_type=jnp.float32))
    queries = query_f.astype(jnp.bfloat16)
    key_flat = key_f.astype(jnp.bfloat16)
    value_flat = jnp.dot(normed, w_value, preferred_element_type=jnp.float32).astype(jnp.bfloat16)
    query_heads = queries.reshape(row_count, HEADS, HEAD_DIM)
    pattern_row = block_pattern[0]
    start_state = (
        jnp.zeros((row_count, HEADS, HEAD_DIM), jnp.float32),
        jnp.zeros((row_count, HEADS), jnp.float32),
    )
    fold_step = partial(
        attend_piece,
        query_heads=query_heads,
        query_labels=node_cluster,
        pattern_row=pattern_row,
        skip_empty=False,
    )
    key_set = None
    key_set = (
        lax.all_gather(key_flat, "blk", axis=0, tiled=True),
        lax.all_gather(value_flat, "blk", axis=0, tiled=True),
        lax.all_gather(node_cluster, "blk", axis=0, tiled=True),
    )
    numer, denom = fold_step(start_state, key_set, 0)
    slot_table = incoming.reshape(peer_count * slot_count, feat_width)
    pair_index = edge_src * row_count + edge_dst
    edge_counts = jnp.zeros((peer_count * slot_count * row_count,), jnp.int32).at[pair_index].add(1)
    edge_counts = edge_counts.reshape(peer_count * slot_count, row_count).astype(jnp.bfloat16)
    degree = jnp.maximum(
        jax.ops.segment_sum(jnp.ones(edge_dst.shape, jnp.float32), edge_dst, row_count), 1.0
    )
    neighbour_sum = jnp.einsum(
        "sr,sd->rd", edge_counts, slot_table, preferred_element_type=jnp.float32
    )
    mean_rows = (neighbour_sum / degree[:, None]).astype(jnp.bfloat16)
    local_term = jnp.dot(mean_rows, w_message, preferred_element_type=jnp.float32)
    attn_heads = (numer / denom[..., None]).astype(jnp.bfloat16)
    attn_rows = attn_heads.reshape(row_count, feat_width)
    attn_proj = jnp.dot(attn_rows, w_out, preferred_element_type=jnp.float32)
    layer_out = (features + local_term + attn_proj).astype(jnp.bfloat16)
    grad_attn = jnp.einsum(
        "rd,ed->re", out_grad, w_out, preferred_element_type=jnp.float32
    ).reshape(row_count, HEADS, HEAD_DIM)
    grad_heads = (grad_attn / denom[..., None]).astype(jnp.bfloat16)
    correction = jnp.sum(grad_attn * attn_heads.astype(jnp.float32), axis=-1) / denom
    key_rows, value_rows, key_labels = key_set
    block_inputs = (
        key_rows.reshape(block_count, row_count, HEADS, HEAD_DIM),
        value_rows.reshape(block_count, row_count, HEADS, HEAD_DIM),
        key_labels.reshape(block_count, row_count),
        pattern_row,
    )
    block_step = partial(key_block, query_heads, grad_heads, correction, node_cluster, False)
    dq_heads, (key_terms, value_terms) = lax.scan(
        block_step, jnp.zeros((row_count, HEADS, HEAD_DIM), jnp.float32), block_inputs
    )
    key_grad, value_grad = (
        lax.psum_scatter(
            key_terms.reshape(block_count * row_count, feat_width).astype(jnp.bfloat16),
            "blk",
            scatter_dimension=0,
            tiled=True,
        ).astype(jnp.float32),
        lax.psum_scatter(
            value_terms.reshape(block_count * row_count, feat_width).astype(jnp.bfloat16),
            "blk",
            scatter_dimension=0,
            tiled=True,
        ).astype(jnp.float32),
    )
    dq_flat = dq_heads.reshape(row_count, feat_width)
    dquery = query_pull(dq_flat)[0].astype(jnp.bfloat16)
    dkey = key_pull(key_grad)[0].astype(jnp.bfloat16)
    dvalue = value_grad.astype(jnp.bfloat16)
    dmessage = (
        jnp.einsum("rd,ed->re", out_grad, w_message, preferred_element_type=jnp.float32)
        / degree[:, None]
    ).astype(jnp.bfloat16)
    slot_grads = jnp.dot(edge_counts, dmessage, preferred_element_type=jnp.float32).astype(
        jnp.bfloat16
    )
    returned = lax.all_to_all(
        slot_grads.reshape(peer_count, slot_count, feat_width),
        "dom",
        split_axis=0,
        concat_axis=0,
        tiled=True,
    )
    returned = jnp.where(live_slots[:, :, None], returned.astype(jnp.float32), 0.0)
    halo_grad = jax.ops.segment_sum(
        returned.reshape(peer_count * slot_count, feat_width), send_rows.reshape(-1), row_count
    )
    dnormed = jnp.einsum("rd,ed->re", dquery, w_query, preferred_element_type=jnp.float32)
    dnormed = dnormed + jnp.einsum("rd,ed->re", dkey, w_key, preferred_element_type=jnp.float32)
    dnormed = dnormed + jnp.einsum("rd,ed->re", dvalue, w_value, preferred_element_type=jnp.float32)
    dnormed = dnormed + halo_grad
    dfeatures, gain_term = norm_pull(dnormed)
    feature_grad = (out_grad.astype(jnp.float32) + dfeatures).astype(jnp.bfloat16)
    weight_terms = jnp.stack(
        [
            jnp.einsum("rd,re->de", normed, dquery, preferred_element_type=jnp.float32),
            jnp.einsum("rd,re->de", normed, dkey, preferred_element_type=jnp.float32),
            jnp.einsum("rd,re->de", normed, dvalue, preferred_element_type=jnp.float32),
            jnp.einsum("rd,re->de", attn_rows, out_grad, preferred_element_type=jnp.float32),
            jnp.einsum("rd,re->de", mean_rows, out_grad, preferred_element_type=jnp.float32),
        ]
    )
    weight_sums, gain_sum = lax.psum((weight_terms, gain_term), ("dom", "blk"))
    return (layer_out, feature_grad, weight_sums, gain_sum)


def solution(mesh):
    placed = (
        P(("dom", "blk"), None),
        P(),
        P(),
        P(),
        P(),
        P(),
        P(),
        P(("dom", "blk")),
        P(("dom", "blk"), None),
        P(("dom", "blk"), None),
        P(("dom", "blk")),
        P(("dom", "blk")),
        P(("dom", "blk")),
        P(("dom", "blk"), None),
    )
    return jax.shard_map(
        local,
        mesh=mesh,
        in_specs=placed,
        out_specs=(P(("dom", "blk"), None), P(("dom", "blk"), None), P(), P()),
        check_vma=False,
    )
```

profile of v0, /device:TPU:1, one launch (start us, length us, event | category | flops | bytes accessed | tf_op | source)
XLA Modules:
  0.0 467.6 jit_solution(4525256311109926087)
XLA Ops:
  15.0 2.1 copy.152
  18.3 13.1 %all-gather = s32[8,1,256]{2,1,0:T(1,128)S(1)} all-gather(s32[1,1,256]{2,1,0:T(1,128)S(1)} %bitcast.258), channel_id=1, replica_groups=mesh['dom'=16,'blk'=8] {'blk'}, dimensions={0}, use_global_device_ids=true | all-gather | bytes 9216 | tf_op jit(solution)/shard_map/all_gather | solution.py:156
  31.7 1.5 compare_and_fusion.1
  33.6 7.9 %all-gather.6.cloned.1.call-done = bf16[2048,512]{1,0:T(8,128)(2,1)} async-done(((bf16[256,512]{1,0:T(8,128)(2,1)}), bf16[2048,512]{1,0:T(8,128)(2,1)}) %all-gather.6.cloned.1.call-update) | async-done | bytes 2097168 | tf_op jit(solution)/shard_map/all_gather | solution.py:154
  41.5 2.5 fusion.54
  43.9 1.8 copy.156
  45.7 23.3 %all-gather.4.cloned.1.call-done = bf16[2048,512]{1,0:T(8,128)(2,1)} async-done(((bf16[256,512]{1,0:T(8,128)(2,1)}), bf16[2048,512]{1,0:T(8,128)(2,1)}) %all-gather.4.cloned.1.call-update) | async-done | bytes 2097168 | tf_op jit(solution)/shard_map/all_gather | solution.py:155
  69.0 2.8 fusion.55
  71.9 1.8 copy.150
  83.3 1.8 copy.174
  85.1 1.8 copy.173
  86.9 1.8 copy.177
  88.7 1.8 copy.176
  90.5 1.8 fusion.64
  101.9 6.1 %reshape.794 = bf16[8,256,8,64]{3,2,1,0:T(8,128)(2,1)} reshape(bf16[2048,512]{1,0:T(8,128)(2,1)} %all-gather.6.cloned.1.call-done) | data formatting | bytes 4194304 | tf_op jit(solution)/shard_map/reshape | solution.py:182
  108.0 5.1 %copy.182 = bf16[8,256,8,64]{1,3,2,0:T(8,128)(2,1)} copy(bf16[8,256,8,64]{3,2,1,0:T(8,128)(2,1)} %reshape.794) | data formatting | bytes 4194304
  113.1 6.1 %reshape.795 = bf16[8,256,8,64]{3,2,1,0:T(8,128)(2,1)} reshape(bf16[2048,512]{1,0:T(8,128)(2,1)} %all-gather.4.cloned.1.call-done) | data formatting | bytes 4194304 | tf_op jit(solution)/shard_map/reshape | solution.py:183
  119.3 5.1 %copy.183 = bf16[8,256,8,64]{1,3,2,0:T(8,128)(2,1)} copy(bf16[8,256,8,64]{3,2,1,0:T(8,128)(2,1)} %reshape.795) | data formatting | bytes 4194304
  124.4 67.0 %while.17 = (s32[]{:T(128)}, f32[256,8,64]{0,2,1:T(8,128)S(1)}, bf16[8,256,512]{1,2,0:T(8,128)(2,1)}, bf16[8,256,512]{2,1,0:T(8,128)(2,1)}, bf16[8,256,8,64]{1,3...) while((s32[]{:T(128)}, f32[256,8,64]{0,2,1:T(8,128)S(1)}, ...), condition=%wide.region_23.24_spmd.clone, body=%wide.region_22.23_spmd.clone.sunk | while | flops 340262912 | bytes 15088305 | solution.py:188
  125.8 1.6 bitcast_select_fusion.2
  134.1 1.6 bitcast_select_fusion.2
  142.5 1.6 bitcast_select_fusion.2
  150.9 1.6 bitcast_select_fusion.2
  159.2 1.6 bitcast_select_fusion.2
  167.6 1.6 bitcast_select_fusion.2
  176.0 1.6 bitcast_select_fusion.2
  184.4 1.6 bitcast_select_fusion.2
  191.4 4.0 copy.184
  196.1 7.5 %gather_fusion = bf16[2048,512]{1,0:T(8,128)(2,1)S(1)} fusion(bf16[256,512]{1,0:T(8,128)(2,1)S(1)} %fusion.38, s32[2048]{0:T(1024)S(1)} %fusion.48), kind=kCustom, calls=%fused_computation | custom fusion | bytes 4202496 | tf_op jit(solution)/shard_map/gather | solution.py:130
  203.7 1.5 broadcast_select_fusion
  205.2 6.6 %all-to-all-start = ((bf16[16,128,512]{2,1,0:T(8,128)(2,1)}), bf16[16,128,512]{2,1,0:T(8,128)(2,1)}, u32[]{:S(2)}, u32[]{:S(2)}) async-start(bf16[16,128,512]{2,1,0:T(8,128)(2,1)} %broadcast_select_fusion), calls=%async_computation | async-start | bytes 4194304 | tf_op jit(solution)/shard_map/all_to_all | solution.py:131
  212.6 22.4 %scatter_custom_fusion = s32[524288]{0:T(1024)S(1)} fusion(s32[4096]{0:T(1024)S(1)} %compare_select_fusion, s32[4096]{0:T(1024)S(1)} %broadcast.736, s32[]{:T(128)} %constant.148.clone.1), kind=kCustom, calls=%fused_computation.77 | custom fusion | flops 4096 | bytes 2097156 | tf_op jit(solution)/shard_map/scatter-add | solution.py:161
  236.1 1.5 convert_element_type.131
  237.6 28.8 %scatter_custom_fusion.1 = f32[256]{0:T(256)S(1)} fusion(s32[4096]{0:T(1024)S(1)} %copy-done.48, f32[4096]{0:T(1024)S(1)} %broadcast.737, f32[]{:T(128)} %constant.152.clone.1), kind=kCustom, calls=%fused_computation.188 | custom fusion | flops 4096 | bytes 1028 | tf_op jit(solution)/shard_map/scatter-add | solution.py:164
  266.4 2.4 convolution_convert_fusion
  268.8 6.6 %all-to-all-start.1 = ((bf16[16,128,512]{2,1,0:T(8,128)(2,1)}), bf16[16,128,512]{2,1,0:T(8,128)(2,1)S(1)}, u32[]{:S(2)}, u32[]{:S(2)}) async-start(bf16[16,128,512]{2,1,0:T(8,128)(2,1)} %bitcast.233), calls=%async_computation.3 | async-start | bytes 4194304 | tf_op jit(solution)/shard_map/all_to_all | solution.py:216
  275.4 3.4 fusion.21
  281.1 2.0 convert_multiply_fusion.4
  283.1 2.1 copy.186
  287.1 2.0 copy.187
  289.2 1.5 fusion.41
  292.7 2.3 fusion.16
  299.7 2.5 all-to-all-done.1
  302.2 2.5 convert_select_fusion
  306.9 13.5 %scatter_fusion = f32[256,512]{1,0:T(8,128)S(1)} fusion(f32[256,512]{1,0:T(8,128)S(1)} %convolution_add_fusion.7, s32[2048]{0:T(1024)S(1)} %bitcast.259, f32[2048,512]{1,0:T(8,128)} %bitcast.218), kind=kCustom, calls=%fused_computation.3 | custom fusion | flops 1048576 | bytes 12591104 | tf_op jit(solution)/shard_map/scatter-add | solution.py:224
  320.6 65.8 %psum.15 = f32[512]{0:T(512)} all-reduce(f32[512]{0:T(512)S(1)} %get-tuple-element.245), channel_id=1, replica_groups=mesh['dom'=16,'blk'=8] {'dom','blk'}, use_global_device_ids=true, to_apply=%region_32.33 | all-reduce | flops 512 | bytes 4096 | tf_op jit(solution)/shard_map/psum | solution.py:242
  387.3 67.9 %all-reduce.2.cloned.1.call-done = f32[5,512,512]{2,1,0:T(8,128)} async-done(((f32[5,512,512]{2,1,0:T(8,128)}), f32[5,512,512]{2,1,0:T(8,128)}) %all-reduce.2.cloned.1.call-update) | async-done | bytes 5242896 | tf_op jit(solution)/shard_map/psum | solution.py:242
  455.3 5.8 %copy.248 = f32[5,512,512]{2,1,0:T(8,128)} copy(f32[5,512,512]{2,1,0:T(8,128)} %all-reduce.2.cloned.1.call-done) | data formatting | bytes 10485760
  (293 shorter events, 93.4 us)
Async XLA Ops:
  7.2 259.2 %copy-start = (bf16[512,512]{1,0:T(8,128)(2,1)S(1)}, bf16[512,512]{1,0:T(8,128)(2,1)}, u32[]{:S(2)}) copy-start(bf16[512,512]{1,0:T(8,128)(2,1)} %param.22) | copy-start | bytes 1572868
  7.2 34.3 %all-gather.6.cloned.1.call-start = ((), (), s32[]{:S(2)}) async-start(), calls=%async_computation.5 | async-start | bytes 2359296 | tf_op jit(solution)/shard_map/all_gather | solution.py:154
  10.8 1.5 copy-start.1
  11.0 1.3 copy-start.19
  11.1 2.3 copy-start.21
  11.4 2.1 copy-start.6
  12.3 56.8 %all-gather.4.cloned.1.call-start = ((), (), s32[]{:S(2)}) async-start(), calls=%async_computation.4 | async-start | bytes 2359296 | tf_op jit(solution)/shard_map/all_gather | solution.py:155
  13.4 267.7 %reduce-scatter.3.cloned.1.call-start = ((), (), s32[]{:S(2)}) async-start(), calls=%async_computation.6 | async-start | bytes 2359296 | tf_op jit(solution)/shard_map/reduce_scatter | solution.py:192
  14.0 3.1 copy-start.3
  14.0 4.3 copy-start.44
  14.0 17.5 %copy-start.49 = (s32[1,8]{1,0:T(1,128)S(1)}, s32[1,8]{1,0:T(1,128)}, u32[]{:S(2)}) copy-start(s32[1,8]{1,0:T(1,128)} %param.24) | copy-start | bytes 100
  14.1 19.2 %copy-start.7 = (bf16[256,512]{1,0:T(8,128)(2,1)S(1)}, bf16[256,512]{1,0:T(8,128)(2,1)}, u32[]{:S(2)}) copy-start(bf16[256,512]{1,0:T(8,128)(2,1)} %param.29) | copy-start | bytes 786436
  14.1 19.2 %copy-start.17 = (bf16[512,512]{1,0:T(8,128)(2,1)S(1)}, bf16[512,512]{1,0:T(8,128)(2,1)}, u32[]{:S(2)}) copy-start(bf16[512,512]{1,0:T(8,128)(2,1)} %param.21) | copy-start | bytes 1572868
  90.5 1.8 copy-start.24
  90.5 2.1 copy-start.37
  90.5 2.1 copy-start.43
  93.4 1.0 copy-start.35
  93.4 1.0 copy-start.41
  94.3 1.0 copy-start.34
  94.3 1.0 copy-start.40
  95.1 1.0 copy-start.33
  95.2 1.0 copy-start.39
  96.0 1.0 copy-start.32
  96.9 1.0 copy-start.31
  99.8 1.0 copy-start.30
  196.1 7.5 %copy-start.50 = (s32[16]{0:T(128)S(1)}, s32[16]{0:T(128)}, u32[]{:S(2)}) copy-start(s32[16]{0:T(128)} %param.26) | copy-start | bytes 196
  205.2 63.5 %all-to-all-start = ((bf16[16,128,512]{2,1,0:T(8,128)(2,1)}), bf16[16,128,512]{2,1,0:T(8,128)(2,1)}, u32[]{:S(2)}, u32[]{:S(2)}) async-start(bf16[16,128,512]{2,1,0:T(8,128)(2,1)} %broadcast_select_fusion), calls=%async_computation | async-start | bytes 4194304 | tf_op jit(solution)/shard_map/all_to_all | solution.py:131
  211.8 80.8 %reduce-scatter.5.cloned.1.call-start = ((), (), s32[]{:S(2)}) async-start(), calls=%async_computation.7 | async-start | bytes 2359296 | tf_op jit(solution)/shard_map/reduce_scatter | solution.py:198
  236.1 30.3 %copy-start.8 = (bf16[256,512]{1,0:T(8,128)(2,1)S(1)}, bf16[256,512]{1,0:T(8,128)(2,1)}, u32[]{:S(2)}) copy-start(bf16[256,512]{1,0:T(8,128)(2,1)} %param.29) | copy-start | bytes 786436
  237.5 31.2 %copy-start.25 = (bf16[2048,256]{1,0:T(8,128)(2,1)}, bf16[2048,256]{1,0:T(8,128)(2,1)S(1)}, u32[]{:S(2)}) copy-start(bf16[2048,256]{1,0:T(8,128)(2,1)S(1)} %convert_element_type.131) | copy-start | bytes 3145732
  268.8 33.4 %all-to-all-start.1 = ((bf16[16,128,512]{2,1,0:T(8,128)(2,1)}), bf16[16,128,512]{2,1,0:T(8,128)(2,1)S(1)}, u32[]{:S(2)}, u32[]{:S(2)}) async-start(bf16[16,128,512]{2,1,0:T(8,128)(2,1)} %bitcast.233), calls=%async_computation.3 | async-start | bytes 4194304 | tf_op jit(solution)/shard_map/all_to_all | solution.py:216
  275.4 179.9 %all-reduce.2.cloned.1.call-start = ((), (), s32[]{:S(2)}) async-start(), calls=%async_computation.8 | async-start | bytes 10485760 | tf_op jit(solution)/shard_map/psum | solution.py:242
  275.4 3.4 copy-start.4
  281.1 8.1 %copy-start.2 = (f32[256,512]{1,0:T(8,128)S(1)}, f32[256,512]{1,0:T(8,128)}, u32[]{:S(2)}) copy-start(f32[256,512]{1,0:T(8,128)} %copy-done.1) | copy-start | bytes 1572868
  291.4 3.6 copy-start.9
  291.4 3.6 copy-start.27
  292.7 3.6 copy-start.28
  297.5 1.0 copy-start.29
  299.7 5.1 %copy-start.12 = (bf16[256,8,64]{0,2,1:T(8,128)(2,1)S(1)}, bf16[256,8,64]{0,2,1:T(8,128)(2,1)}, u32[]{:S(2)}) copy-start(bf16[256,8,64]{0,2,1:T(8,128)(2,1)} %copy-done.11) | copy-start | bytes 786436
  302.2 2.5 copy-start.22
  302.2 2.9 copy-start.16
  302.2 2.9 copy-start.18
  304.7 1.4 copy-start.14
  304.7 1.4 copy-start.15
  304.7 1.8 copy-start.20
  304.7 1.8 copy-start.26
  306.9 13.6 %copy-start.46 = (f32[512]{0:T(512)S(1)}, f32[512]{0:T(512)}, u32[]{:S(2)}) copy-start(f32[512]{0:T(512)} %param.17) | copy-start | bytes 6148
  306.9 79.6 %copy-start.10 = (bf16[256,512]{1,0:T(8,128)(2,1)S(1)}, bf16[256,512]{1,0:T(8,128)(2,1)}, u32[]{:S(2)}) copy-start(bf16[256,512]{1,0:T(8,128)(2,1)} %param.29) | copy-start | bytes 786436
  (10 other events, 8.3 us)
Sparse Core Ops, SparseCore 0:
  12.4 29.0 all-gather.5
  43.2 25.8 all-gather.3
  195.5 30.9 reduce-scatter.2
  228.8 32.8 reduce-scatter.4
  297.7 157.5 all-reduce.1
where the time goes:
time: 470 us; the launch traced here: 468 us
  waiting for transfers between devices  102 us (22%)
  local copies, waits for them, and re-layouts  97.6 us (21%)
  other arithmetic  84.2 us (18%)
  blocking collectives  78.9 us (17%)
  matrix products  70.8 us (15%)
  between operations  14.7 us (3%)
  starting transfers between devices  13.4 us (3%)
  loops' own time  5.81 us (1%)
    psum x1, waiting for transfers between devices, local(): weight_sums, gain_sum = lax.psum((weight_terms, gain_term), ('dom', 'blk'))  67.9 us
    psum x1, blocking collectives, local(): weight_sums, gain_sum = lax.psum((weight_terms, gain_term), ('dom', 'blk'))  65.8 us
    scatter-add x1, other arithmetic, local(): jax.ops.segment_sum(jnp.ones(edge_dst.shape, jnp.float32), edge_dst, row_...  28.8 us
    all_gather x1, waiting for transfers between devices, local(): lax.all_gather(value_flat, 'blk', axis=0, tiled=True)  23.3 us
    scatter-add x1, other arithmetic, local(): jnp.zeros((peer_count * slot_count * row_count,), jnp.int32).at[pair_index]  22.4 us
    unnamed x106, local copies, waits for them, and re-layouts  20.3 us
    dot_general x16, matrix products, block_weights(): jnp.einsum('rhe,khe->hrk', query_heads, key_heads, preferred_element_type...  19.7 us
    slice x9, local copies, waits for them, and re-layouts, attend_piece(): value_rows[first_row:last_row].reshape(part_rows, HEADS, HEAD_DIM)  13.6 us
  transfers between devices with their start and end apart: 7, of which 4 were waited for; matrix products, arithmetic and copies ran while one was open for 25% of the time, Pallas kernels for 0%

commit v1 on v0

--- a/solution.py
+++ b/solution.py
@@ -8,6 +8,19 @@
 HEAD_DIM = 64
 epsilon = 1e-06
 score_shift = 8.0
+
+
+def collect(x, axis, dim):
+    ways = lax.axis_size(axis)
+    up = [(d, (d + 1) % ways) for d in range(ways)]
+    down = [(d, (d - 1) % ways) for d in range(ways)]
+    earlier, later = ([x], [x])
+    for _ in range(ways // 2):
+        earlier.append(lax.ppermute(earlier[-1], axis, up))
+    for _ in range((ways - 1) // 2):
+        later.append(lax.ppermute(later[-1], axis, down))
+    line = jnp.concatenate([*earlier[::-1], *later[1:]], axis=dim)
+    return jnp.roll(line, (lax.axis_index(axis) - ways // 2) * x.shape[dim], axis=dim)
 
 
 def settle(array):
@@ -152,7 +165,7 @@
     key_set = None
     key_set = (
         lax.all_gather(key_flat, "blk", axis=0, tiled=True),
-        lax.all_gather(value_flat, "blk", axis=0, tiled=True),
+        collect(value_flat, "blk", 0),
         lax.all_gather(node_cluster, "blk", axis=0, tiled=True),
     )
     numer, denom = fold_step(start_state, key_set, 0)

time: 470 us -> 476 us (1.013)
  waiting for transfers between devices: 102 us -> 76.8 us
  local copies, waits for them, and re-layouts: 97.6 us -> 111 us
  starting transfers between devices: 13.4 us -> 23.8 us
    all_gather x1 -> x0, waiting for transfers between devices: 23.3 us -> none  [local(): lax.all_gather(value_flat, 'blk', axis=0, tiled=True)]
    unnamed x106 -> x129, local copies, waits for them, and re-layouts: 20.3 us -> 32 us
    ppermute x0 -> x7, starting transfers between devices: none -> 10.5 us  [the longest x4 7.28 us: collect(): earlier.append(lax.ppermute(earlier[-1], axis, up))]
    all_gather x1, waiting for transfers between devices: 7.86 us -> 0.01 us  [local(): lax.all_gather(key_flat, 'blk', axis=0, tiled=True)]
    ppermute x0 -> x7, waiting for transfers between devices: none -> 7.73 us  [the longest x4 7.73 us: collect(): earlier.append(lax.ppermute(earlier[-1], axis, up))]
  transfers between devices with their start and end apart: 7 -> 13, of which waited for: 4 -> 2; matrix products, arithmetic and copies ran while one was open for 25% -> 33% of each run, Pallas kernels for 0% -> 0%
where the time goes in v1:
time: 476 us; the launch traced here: 473 us
  local copies, waits for them, and re-layouts  111 us (23%)
  other arithmetic  88.7 us (19%)
  blocking collectives  81.7 us (17%)
  waiting for transfers between devices  76.8 us (16%)
  matrix products  70 us (15%)
  starting transfers between devices  23.8 us (5%)
  between operations  14.9 us (3%)
  loops' own time  5.81 us (1%)
    psum x1, blocking collectives, local(): weight_sums, gain_sum = lax.psum((weight_terms, gain_term), ('dom', 'blk'))  69.8 us
    psum x1, waiting for transfers between devices, local(): weight_sums, gain_sum = lax.psum((weight_terms, gain_term), ('dom', 'blk'))  68.3 us
    unnamed x129, local copies, waits for them, and re-layouts  32 us
    scatter-add x1, other arithmetic, local(): jax.ops.segment_sum(jnp.ones(edge_dst.shape, jnp.float32), edge_dst, row_...  28.8 us
    scatter-add x1, other arithmetic, local(): jnp.zeros((peer_count * slot_count * row_count,), jnp.int32).at[pair_index]  22.4 us
    dot_general x16, matrix products, block_weights(): jnp.einsum('rhe,khe->hrk', query_heads, key_heads, preferred_element_type...  19.7 us
    slice x9, local copies, waits for them, and re-layouts, attend_piece(): key_part = key_rows[first_row:last_row].reshape(part_rows, HEADS, HEAD_DIM)  14.1 us
    scatter-add x1, other arithmetic, local(): jax.ops.segment_sum(returned.reshape(peer_count * slot_count, feat_width)...  13.4 us
  transfers between devices with their start and end apart: 13, of which 2 were waited for; matrix products, arithmetic and copies ran while one was open for 33% of the time, Pallas kernels for 0%

profile of v1, /device:TPU:1, one launch (start us, length us, event | category | flops | bytes accessed | tf_op | source)
XLA Modules:
  0.0 473.2 jit_solution(1638827338240900291)
XLA Ops:
  10.9 3.0 collective-permute-start
  20.3 11.9 %all-gather = s32[8,1,256]{2,1,0:T(1,128)S(1)} all-gather(s32[1,1,256]{2,1,0:T(1,128)S(1)} %bitcast.258), channel_id=1, replica_groups=mesh['dom'=16,'blk'=8] {'blk'}, dimensions={0}, use_global_device_ids=true | all-gather | bytes 9216 | tf_op jit(solution)/shard_map/all_gather | solution.py:169
  32.3 7.7 %collective-permute-done.1 = bf16[256,512]{1,0:T(8,128)(2,1)} collective-permute-done((bf16[256,512]{1,0:T(8,128)(2,1)}, bf16[256,512]{1,0:T(8,128)(2,1)}, u32[]{:S(2)}, u32[]{:S(2)}) %collective-permute-start.1) | collective-permute-done | bytes 262176 | tf_op jit(solution)/shard_map/ppermute | solution.py:19
  40.1 2.5 collective-permute-start.2
  46.9 1.7 collective-permute-start.3
  48.6 2.2 compare_and_fusion.1
  52.4 2.2 collective-permute-start.6
  67.9 1.8 copy.149
  69.7 1.8 copy.160
  71.5 1.8 copy.163
  76.1 3.1 constant_dynamic-slice_fusion.9
  79.1 6.1 %reshape.795 = bf16[8,256,8,64]{3,2,1,0:T(8,128)(2,1)} reshape(bf16[2048,512]{1,0:T(8,128)(2,1)} %constant_dynamic-slice_fusion.9) | data formatting | bytes 4194304 | tf_op jit(solution)/shard_map/reshape | solution.py:196
  85.3 5.2 %copy.182 = bf16[8,256,8,64]{1,3,2,0:T(8,128)(2,1)} copy(bf16[8,256,8,64]{3,2,1,0:T(8,128)(2,1)} %reshape.795) | data formatting | bytes 4194304
  90.4 2.6 fusion.54
  93.0 1.8 copy.158
  94.8 1.8 copy.155
  96.6 1.8 copy.161
  98.4 1.8 copy.164
  100.2 1.8 copy.167
  104.5 1.7 fusion.64
  116.8 6.1 %reshape.794 = bf16[8,256,8,64]{3,2,1,0:T(8,128)(2,1)} reshape(bf16[2048,512]{1,0:T(8,128)(2,1)} %all-gather.3.cloned.1.call-done) | data formatting | bytes 4194304 | tf_op jit(solution)/shard_map/reshape | solution.py:195
  123.0 5.1 %copy.181 = bf16[8,256,8,64]{1,3,2,0:T(8,128)(2,1)} copy(bf16[8,256,8,64]{3,2,1,0:T(8,128)(2,1)} %reshape.794) | data formatting | bytes 4194304
  128.1 67.0 %while.17 = (s32[]{:T(128)}, f32[256,8,64]{0,2,1:T(8,128)S(1)}, bf16[8,256,512]{1,2,0:T(8,128)(2,1)}, bf16[8,256,512]{2,1,0:T(8,128)(2,1)}, bf16[8,256,8,64]{1,3...) while((s32[]{:T(128)}, f32[256,8,64]{0,2,1:T(8,128)S(1)}, ...), condition=%wide.region_23.24_spmd.clone, body=%wide.region_22.23_spmd.clone.sunk | while | flops 340262912 | bytes 15088305 | solution.py:201
  129.4 1.6 bitcast_select_fusion.2
  137.8 1.6 bitcast_select_fusion.2
  146.2 1.6 bitcast_select_fusion.2
  154.6 1.6 bitcast_select_fusion.2
  163.0 1.6 bitcast_select_fusion.2
  171.3 1.6 bitcast_select_fusion.2
  179.7 1.6 bitcast_select_fusion.2
  188.1 1.6 bitcast_select_fusion.2
  195.0 4.2 copy.183
  199.9 7.5 %gather_fusion = bf16[2048,512]{1,0:T(8,128)(2,1)S(1)} fusion(bf16[256,512]{1,0:T(8,128)(2,1)S(1)} %fusion.38, s32[2048]{0:T(1024)S(1)} %fusion.48), kind=kCustom, calls=%fused_computation | custom fusion | bytes 4202496 | tf_op jit(solution)/shard_map/gather | solution.py:143
  209.0 6.6 %all-to-all-start = ((bf16[16,128,512]{2,1,0:T(8,128)(2,1)}), bf16[16,128,512]{2,1,0:T(8,128)(2,1)}, u32[]{:S(2)}, u32[]{:S(2)}) async-start(bf16[16,128,512]{2,1,0:T(8,128)(2,1)} %broadcast_select_fusion), calls=%async_computation | async-start | bytes 4194304 | tf_op jit(solution)/shard_map/all_to_all | solution.py:144
  216.4 22.4 %scatter_custom_fusion = s32[524288]{0:T(1024)S(1)} fusion(s32[4096]{0:T(1024)S(1)} %compare_select_fusion, s32[4096]{0:T(1024)S(1)} %broadcast.737, s32[]{:T(128)} %constant.171.clone.1), kind=kCustom, calls=%fused_computation.77 | custom fusion | flops 4096 | bytes 2097156 | tf_op jit(solution)/shard_map/scatter-add | solution.py:174
  241.5 28.8 %scatter_custom_fusion.1 = f32[256]{0:T(256)S(1)} fusion(s32[4096]{0:T(1024)S(1)} %copy-done.52, f32[4096]{0:T(1024)S(1)} %broadcast.738, f32[]{:T(128)} %constant.175.clone.1), kind=kCustom, calls=%fused_computation.213 | custom fusion | flops 4096 | bytes 1028 | tf_op jit(solution)/shard_map/scatter-add | solution.py:177
  270.3 2.4 convolution_convert_fusion
  272.6 6.6 %all-to-all-start.1 = ((bf16[16,128,512]{2,1,0:T(8,128)(2,1)}), bf16[16,128,512]{2,1,0:T(8,128)(2,1)S(1)}, u32[]{:S(2)}, u32[]{:S(2)}) async-start(bf16[16,128,512]{2,1,0:T(8,128)(2,1)} %bitcast.233), calls=%async_computation.3 | async-start | bytes 4194304 | tf_op jit(solution)/shard_map/all_to_all | solution.py:229
  279.3 3.4 fusion.21
  284.9 2.1 convert_multiply_fusion.4
  287.0 2.1 copy.185
  291.1 2.1 copy.186
  296.6 2.3 fusion.16
  303.7 2.3 convert_select_fusion
  308.2 13.4 %scatter_fusion = f32[256,512]{1,0:T(8,128)S(1)} fusion(f32[256,512]{1,0:T(8,128)S(1)} %convolution_add_fusion.7, s32[2048]{0:T(1024)S(1)} %bitcast.259, f32[2048,512]{1,0:T(8,128)} %bitcast.218), kind=kCustom, calls=%fused_computation.3 | custom fusion | flops 1048576 | bytes 12591104 | tf_op jit(solution)/shard_map/scatter-add | solution.py:237
  321.8 69.8 %psum.15 = f32[512]{0:T(512)} all-reduce(f32[512]{0:T(512)S(1)} %get-tuple-element.245), channel_id=1, replica_groups=mesh['dom'=16,'blk'=8] {'dom','blk'}, use_global_device_ids=true, to_apply=%region_32.33 | all-reduce | flops 512 | bytes 4096 | tf_op jit(solution)/shard_map/psum | solution.py:255
  392.6 68.3 %all-reduce.2.cloned.1.call-done = f32[5,512,512]{2,1,0:T(8,128)} async-done(((f32[5,512,512]{2,1,0:T(8,128)}), f32[5,512,512]{2,1,0:T(8,128)}) %all-reduce.2.cloned.1.call-update) | async-done | bytes 5242896 | tf_op jit(solution)/shard_map/psum | solution.py:255
  460.8 5.8 %copy.262 = f32[5,512,512]{2,1,0:T(8,128)} copy(f32[5,512,512]{2,1,0:T(8,128)} %all-reduce.2.cloned.1.call-done) | data formatting | bytes 10485760
  (329 shorter events, 114.2 us)
Async XLA Ops:
  7.2 263.1 %copy-start = (bf16[512,512]{1,0:T(8,128)(2,1)S(1)}, bf16[512,512]{1,0:T(8,128)(2,1)}, u32[]{:S(2)}) copy-start(bf16[512,512]{1,0:T(8,128)(2,1)} %param.22) | copy-start | bytes 1572868
  7.2 6.7 %copy-start.16 = (bf16[512,512]{1,0:T(8,128)(2,1)S(1)}, bf16[512,512]{1,0:T(8,128)(2,1)}, u32[]{:S(2)}) copy-start(bf16[512,512]{1,0:T(8,128)(2,1)} %param.19) | copy-start | bytes 1572868
  7.2 83.2 %all-gather.3.cloned.1.call-start = ((), (), s32[]{:S(2)}) async-start(), calls=%async_computation.4 | async-start | bytes 2359296 | tf_op jit(solution)/shard_map/all_gather | solution.py:167
  10.9 21.4 %collective-permute-start = (bf16[256,512]{1,0:T(8,128)(2,1)S(1)}, bf16[256,512]{1,0:T(8,128)(2,1)}, u32[]{:S(2)}, u32[]{:S(2)}) collective-permute-start(bf16[256,512]{1,0:T(8,128)(2,1)S(1)} %convolution_convert_fusion.1), channel_id=1, source_target_pairs={{0,1},{1,2},{2,3},{3,4},{4,5},{5,6},{6,7},{7,0},{8,9},{9,10},{10,1... | collective-permute-start | bytes 786440 | tf_op jit(solution)/shard_map/ppermute | solution.py:19
  13.9 32.0 %collective-permute-start.4 = (bf16[256,512]{1,0:T(8,128)(2,1)S(1)}, bf16[256,512]{1,0:T(8,128)(2,1)}, u32[]{:S(2)}, u32[]{:S(2)}) collective-permute-start(bf16[256,512]{1,0:T(8,128)(2,1)S(1)} %convolution_convert_fusion.1), channel_id=1, source_target_pairs={{0,7},{1,0},{2,1},{3,2},{4,3},{5,4},{6,5},{7,6},{8,15},{9,8},{10,9... | collective-permute-start | bytes 786440 | tf_op jit(solution)/shard_map/ppermute | solution.py:21
  14.2 1.4 copy-start.1
  14.4 1.3 copy-start.53
  14.4 4.8 %copy-start.22 = (bf16[512,512]{1,0:T(8,128)(2,1)S(1)}, bf16[512,512]{1,0:T(8,128)(2,1)}, u32[]{:S(2)}) copy-start(bf16[512,512]{1,0:T(8,128)(2,1)} %param.18) | copy-start | bytes 1572868
  14.8 3.9 copy-start.7
  14.8 5.6 %copy-start.48 = (s32[256]{0:T(256)S(1)}, s32[256]{0:T(256)}, u32[]{:S(2)}) copy-start(s32[256]{0:T(256)} %param.23) | copy-start | bytes 3076
  15.7 269.3 %reduce-scatter.3.cloned.1.call-start = ((), (), s32[]{:S(2)}) async-start(), calls=%async_computation.5 | async-start | bytes 2359296 | tf_op jit(solution)/shard_map/reduce_scatter | solution.py:205
  20.3 30.6 %copy-start.3 = (f32[256,512]{0,1:T(8,128)}, f32[256,512]{0,1:T(8,128)S(1)}, u32[]{:S(2)}) copy-start(f32[256,512]{0,1:T(8,128)S(1)} %copy.150) | copy-start | bytes 1572868
  32.2 7.8 %collective-permute-start.1 = (bf16[256,512]{1,0:T(8,128)(2,1)}, bf16[256,512]{1,0:T(8,128)(2,1)}, u32[]{:S(2)}, u32[]{:S(2)}) collective-permute-start(bf16[256,512]{1,0:T(8,128)(2,1)} %collective-permute-done), channel_id=1, source_target_pairs={{0,1},{1,2},{2,3},{3,4},{4,5},{5,6},{6,7},{7,0},{8,9},{9,10},{10,1... | collective-permute-start | bytes 786440 | tf_op jit(solution)/shard_map/ppermute | solution.py:19
  32.3 19.7 %copy-start.8 = (bf16[256,512]{1,0:T(8,128)(2,1)S(1)}, bf16[256,512]{1,0:T(8,128)(2,1)}, u32[]{:S(2)}) copy-start(bf16[256,512]{1,0:T(8,128)(2,1)} %param.29) | copy-start | bytes 786436
  32.3 19.7 %copy-start.19 = (bf16[512,512]{1,0:T(8,128)(2,1)S(1)}, bf16[512,512]{1,0:T(8,128)(2,1)}, u32[]{:S(2)}) copy-start(bf16[512,512]{1,0:T(8,128)(2,1)} %param.21) | copy-start | bytes 1572868
  40.1 6.8 %collective-permute-start.2 = (bf16[256,512]{1,0:T(8,128)(2,1)}, bf16[256,512]{1,0:T(8,128)(2,1)}, u32[]{:S(2)}, u32[]{:S(2)}) collective-permute-start(bf16[256,512]{1,0:T(8,128)(2,1)} %collective-permute-done.1), channel_id=1, source_target_pairs={{0,1},{1,2},{2,3},{3,4},{4,5},{5,6},{6,7},{7,0},{8,9},{9,10},{10,1... | collective-permute-start | bytes 786440 | tf_op jit(solution)/shard_map/ppermute | solution.py:19
  45.9 6.5 %collective-permute-start.5 = (bf16[256,512]{1,0:T(8,128)(2,1)}, bf16[256,512]{1,0:T(8,128)(2,1)S(1)}, u32[]{:S(2)}, u32[]{:S(2)}) collective-permute-start(bf16[256,512]{1,0:T(8,128)(2,1)} %collective-permute-done.4), channel_id=1, source_target_pairs={{0,7},{1,0},{2,1},{3,2},{4,3},{5,4},{6,5},{7,6},{8,15},{9,8},{10,9... | collective-permute-start | bytes 786440 | tf_op jit(solution)/shard_map/ppermute | solution.py:21
  46.9 7.7 %collective-permute-start.3 = (bf16[256,512]{1,0:T(8,128)(2,1)}, bf16[256,512]{1,0:T(8,128)(2,1)}, u32[]{:S(2)}, u32[]{:S(2)}) collective-permute-start(bf16[256,512]{1,0:T(8,128)(2,1)} %collective-permute-done.2), channel_id=1, source_target_pairs={{0,1},{1,2},{2,3},{3,4},{4,5},{5,6},{6,7},{7,0},{8,9},{9,10},{10,1... | collective-permute-start | bytes 786440 | tf_op jit(solution)/shard_map/ppermute | solution.py:19
  52.4 7.1 %collective-permute-start.6 = (bf16[256,512]{1,0:T(8,128)(2,1)S(1)}, bf16[256,512]{1,0:T(8,128)(2,1)S(1)}, u32[]{:S(2)}, u32[]{:S(2)}) collective-permute-start(bf16[256,512]{1,0:T(8,128)(2,1)S(1)} %collective-permute-done.5), channel_id=1, source_target_pairs={{0,7},{1,0},{2,1},{3,2},{4,3},{5,4},{6,5},{7,6},{8,15},{9,8},{10,9... | collective-permute-start | bytes 786440 | tf_op jit(solution)/shard_map/ppermute | solution.py:21
  64.5 2.3 copy-start.6
  104.5 2.1 copy-start.41
  104.5 2.1 copy-start.47
  107.3 1.0 copy-start.39
  109.1 1.0 copy-start.37
  112.7 1.1 copy-start.26
  199.9 7.5 %copy-start.54 = (s32[16]{0:T(128)S(1)}, s32[16]{0:T(128)}, u32[]{:S(2)}) copy-start(s32[16]{0:T(128)} %param.26) | copy-start | bytes 196
  209.0 63.6 %all-to-all-start = ((bf16[16,128,512]{2,1,0:T(8,128)(2,1)}), bf16[16,128,512]{2,1,0:T(8,128)(2,1)}, u32[]{:S(2)}, u32[]{:S(2)}) async-start(bf16[16,128,512]{2,1,0:T(8,128)(2,1)} %broadcast_select_fusion), calls=%async_computation | async-start | bytes 4194304 | tf_op jit(solution)/shard_map/all_to_all | solution.py:144
  215.7 81.0 %reduce-scatter.5.cloned.1.call-start = ((), (), s32[]{:S(2)}) async-start(), calls=%async_computation.6 | async-start | bytes 2359296 | tf_op jit(solution)/shard_map/reduce_scatter | solution.py:211
  240.0 30.3 %copy-start.9 = (bf16[256,512]{1,0:T(8,128)(2,1)S(1)}, bf16[256,512]{1,0:T(8,128)(2,1)}, u32[]{:S(2)}) copy-start(bf16[256,512]{1,0:T(8,128)(2,1)} %param.29) | copy-start | bytes 786436
  241.4 31.2 %copy-start.29 = (bf16[2048,256]{1,0:T(8,128)(2,1)}, bf16[2048,256]{1,0:T(8,128)(2,1)S(1)}, u32[]{:S(2)}) copy-start(bf16[2048,256]{1,0:T(8,128)(2,1)S(1)} %convert_element_type.131) | copy-start | bytes 3145732
  272.6 31.1 %all-to-all-start.1 = ((bf16[16,128,512]{2,1,0:T(8,128)(2,1)}), bf16[16,128,512]{2,1,0:T(8,128)(2,1)S(1)}, u32[]{:S(2)}, u32[]{:S(2)}) async-start(bf16[16,128,512]{2,1,0:T(8,128)(2,1)} %bitcast.233), calls=%async_computation.3 | async-start | bytes 4194304 | tf_op jit(solution)/shard_map/all_to_all | solution.py:229
  279.2 181.6 %all-reduce.2.cloned.1.call-start = ((), (), s32[]{:S(2)}) async-start(), calls=%async_computation.7 | async-start | bytes 10485760 | tf_op jit(solution)/shard_map/psum | solution.py:255
  279.3 3.4 copy-start.4
  284.9 8.2 %copy-start.2 = (f32[256,512]{1,0:T(8,128)S(1)}, f32[256,512]{1,0:T(8,128)}, u32[]{:S(2)}) copy-start(f32[256,512]{1,0:T(8,128)} %copy-done.1) | copy-start | bytes 1572868
  295.3 3.6 copy-start.10
  295.3 3.6 copy-start.31
  296.6 3.6 copy-start.32
  301.5 1.0 copy-start.33
  303.6 2.4 copy-start.13
  303.7 2.3 copy-start.23
  303.7 2.7 copy-start.18
  303.7 2.7 copy-start.20
  306.0 1.4 copy-start.15
  306.0 1.4 copy-start.17
  306.0 1.8 copy-start.21
  306.0 1.8 copy-start.30
  308.1 13.5 %copy-start.50 = (f32[512]{0:T(512)S(1)}, f32[512]{0:T(512)}, u32[]{:S(2)}) copy-start(f32[512]{0:T(512)} %param.17) | copy-start | bytes 6148
  308.2 83.5 %copy-start.11 = (bf16[256,512]{1,0:T(8,128)(2,1)S(1)}, bf16[256,512]{1,0:T(8,128)(2,1)}, u32[]{:S(2)}) copy-start(bf16[256,512]{1,0:T(8,128)(2,1)} %param.29) | copy-start | bytes 786436
  (20 other events, 18.1 us)
Sparse Core Ops, SparseCore 0:
  15.8 28.4 all-gather.2
  199.3 33.8 reduce-scatter.2
  235.6 32.5 reduce-scatter.4
  301.7 159.1 all-reduce.1
